TPU v7x, 32 devices: a whole 2x2x4 slice. The times are simulated.
32 devices in a mesh: mem: 4 (over y, core), sub: 8 (over z, x).
Axes of the slice: x: 2, y: 2, z: 4, core: 2. Of those that a mesh axis runs over, the one named last changes fastest.
Arguments:
- prior_sample_array: float32 [80, 8, 24, 512], P('mem', 'sub'), may hold values from -6 to 6
- courant_x: float32 [8, 512], P('sub'), may hold values from -0.3 to 0.3
- courant_y: float32 [8, 512], P('sub'), may hold values from -0.3 to 0.3
- diffusion: float32 [8, 512], P('sub'), may hold values from 0.02 to 0.09
- obs_cell: int32 [4, 128], replicated, may hold values from 0 to 4095
- obs_value: float32 [4, 128], replicated, may hold values from -6 to 6
- obs_error: float32 [4, 128], replicated, may hold values from 0.2 to 1
- obs_weight: float32 [4, 128, 24], replicated, may hold values from -1.25 to 1.25
- taper_radius: float32 [4, 128], replicated, may hold values from 64 to 256
Outputs:
- analysis: float32 [80, 8, 24, 512], P(None, 'sub', None, 'mem')
All inputs are finite; a program needn't handle non-finite values.
Results may differ from a plain program's by a relative error of at most 0.0003.
Values sent between devices are 32-bit elements; how exact they have to be, the bound alone decides.
No kernel may reach another device: no remote copies, remote signals or barrier semaphores. Data moves between devices by JAX's collectives and lax.ppermute only.
A program may use at most 64 MiB of HBM per device.

v0:
```python
import jax
import jax.numpy as jnp
from jax import lax
from jax.sharding import PartitionSpec as P

highest = lax.Precision.HIGHEST


def padded_2(shard, sides, width):
    for axis, dim in sides:
        size, length = (lax.axis_size(axis), shard.shape[dim])
        up = [(i, (i + 1) % size) for i in range(size - 1)]
        down = [(j, i) for i, j in up]
        last = lax.slice_in_dim(shard, length - width, length, axis=dim)
        first = lax.slice_in_dim(shard, 0, width, axis=dim)
        before = lax.ppermute(last, axis, up)
        after = lax.ppermute(first, axis, down)
        shard = jnp.concatenate([before, shard, after], axis=dim)
    return shard


def gaspari(delta_row, delta_col, cutoff_radius, width):
    cyclic_shifted = (delta_col + width // 2) % width - width // 2
    row_dist = delta_row.astype(jnp.float32)
    col_dist = cyclic_shifted.astype(jnp.float32)
    ratio = jnp.sqrt(row_dist * row_dist + col_dist * col_dist) / cutoff_radius
    inner = (((-0.25 * ratio + 0.5) * ratio + 0.625) * ratio - 5.0 / 3.0) * ratio * ratio + 1.0
    bounded = jnp.maximum(ratio, 1.0)
    outer = (
        ((((ratio / 12.0 - 0.5) * ratio + 0.625) * ratio + 5.0 / 3.0) * ratio - 5.0) * ratio
        + 4.0
        - 2.0 / (3.0 * bounded)
    )
    return jnp.where(ratio <= 1.0, inner, jnp.where(ratio < 2.0, outer, 0.0))


def carried_quantity(
    center,
    west_cells,
    east_cells,
    north_cells,
    southern_neighbours,
    flow_x,
    meridional_velocity,
    mixing,
):
    result = (
        center
        - jnp.maximum(flow_x, 0.0) * (center - west_cells)
        - jnp.minimum(flow_x, 0.0) * (east_cells - center)
    )
    result = (
        result
        - jnp.maximum(meridional_velocity, 0.0) * (center - southern_neighbours)
        - jnp.minimum(meridional_velocity, 0.0) * (north_cells - center)
    )
    return result + mixing * (
        east_cells + west_cells + north_cells + southern_neighbours - 4.0 * center
    )


def obs_factors(obs_prior, obs_value, obs_error):
    members = obs_prior.shape[1]
    average = jnp.mean(obs_prior, axis=1)
    anomaly = obs_prior - average[:, None]
    covariance = jnp.dot(anomaly, anomaly.T, precision=highest) / (members - 1) + jnp.diag(
        obs_error
    )
    factor = jnp.linalg.cholesky(covariance)
    innovation = (obs_value - average)[:, None]
    midpoint_values = lax.linalg.triangular_solve(factor, innovation, left_side=True, lower=True)
    solved = lax.linalg.triangular_solve(
        factor, midpoint_values, left_side=True, lower=True, transpose_a=True
    )
    shifted = factor + jnp.diag(jnp.sqrt(obs_error))
    reduced = lax.linalg.triangular_solve(shifted, anomaly, left_side=True, lower=True)
    squared = lax.linalg.triangular_solve(
        factor, reduced, left_side=True, lower=True, transpose_a=True
    )
    return (anomaly, solved - squared)


def local_prior(existing_grid_values, obs_rows, obs_cols, weights, row_start, col_start):
    rows_dev = existing_grid_values.shape[1]
    cols_dev = existing_grid_values.shape[3]
    local_rows = obs_rows - row_start
    local_cols = obs_cols - col_start
    owned = (
        (local_rows >= 0) & (local_rows < rows_dev) & (local_cols >= 0) & (local_cols < cols_dev)
    )
    picked = existing_grid_values[
        :, jnp.clip(local_rows, 0, rows_dev - 1), :, jnp.clip(local_cols, 0, cols_dev - 1)
    ]
    values = jnp.einsum("kmc,kc->km", picked, weights, precision=highest)
    return jnp.where(owned[:, None], values, 0.0)


def apply_update(existing_grid_values, obs_anomaly, coeffs, taper_cells, members):
    average = jnp.mean(existing_grid_values, axis=0)
    anomaly = existing_grid_values - average[None]
    cross_cov = jnp.einsum("mrcx,km->rcxk", anomaly, obs_anomaly, precision=highest) / (members - 1)
    gain = cross_cov * taper_cells[:, None, :, :]
    return existing_grid_values + jnp.einsum("rcxk,km->mrcx", gain, coeffs, precision=highest)


def shards(
    prior_sample_array,
    courant_x,
    courant_y,
    diffusion,
    obs_cell,
    obs_value,
    obs_error,
    obs_weight,
    taper_radius,
):
    width = courant_x.shape[1]
    rows_dev = prior_sample_array.shape[1]
    cols_dev = width // lax.axis_size("mem")
    members = prior_sample_array.shape[0] * lax.axis_size("mem")
    col_start = lax.axis_index("mem") * cols_dev
    row_start = lax.axis_index("sub") * rows_dev
    padded = padded_2(prior_sample_array, (("sub", 1),), 1)
    propagated_grids = carried_quantity(
        prior_sample_array,
        jnp.roll(prior_sample_array, 1, axis=3),
        jnp.roll(prior_sample_array, -1, axis=3),
        padded[:, 2:],
        padded[:, :-2],
        courant_x[:, None, :],
        courant_y[:, None, :],
        diffusion[:, None, :],
    )
    existing_grid_values = lax.all_to_all(
        propagated_grids, "mem", split_axis=3, concat_axis=0, tiled=True
    )
    row_ids = row_start + jnp.arange(rows_dev, dtype=jnp.int32)
    col_ids = col_start + jnp.arange(cols_dev, dtype=jnp.int32)
    obs_rows = obs_cell // width
    obs_cols = obs_cell % width
    batches = obs_cell.shape[0]

    def taper_cells(batch_index):
        return gaspari(
            row_ids[:, None, None] - obs_rows[batch_index][None, None, :],
            col_ids[None, :, None] - obs_cols[batch_index][None, None, :],
            taper_radius[batch_index][None, None, :],
            width,
        )

    for batch_index in range(batches):
        obs_prior = lax.psum(
            local_prior(
                existing_grid_values,
                obs_rows[batch_index],
                obs_cols[batch_index],
                obs_weight[batch_index],
                row_start,
                col_start,
            ),
            ("mem", "sub"),
        )
        obs_anomaly, coeffs = obs_factors(obs_prior, obs_value[batch_index], obs_error[batch_index])
        existing_grid_values = apply_update(
            existing_grid_values, obs_anomaly, coeffs, taper_cells(batch_index), members
        )
    return existing_grid_values


def solution(mesh):
    return jax.shard_map(
        shards,
        mesh=mesh,
        in_specs=(
            P("mem", "sub", None, None),
            P("sub", None),
            P("sub", None),
            P("sub", None),
            P(),
            P(),
            P(),
            P(),
            P(),
        ),
        out_specs=P(None, "sub", None, "mem"),
        check_vma=False,
    )
```

profile of v0, /device:TPU:0, one launch (start us, length us, event | category | flops | bytes accessed | tf_op | source)
XLA Modules:
  0.0 428.5 jit_solution(3687478982285887635)
XLA Ops:
  0.0 5.9 %collective-permute-start = (f32[20,1,24,512]{3,2,1,0:T(8,128)}, f32[20,1,24,512]{3,2,1,0:T(8,128)}, u32[]{:S(2)}, u32[]{:S(2)}) collective-permute-start(f32[20,1,24,512]{3,2,1,0:T(8,128)} %param.18), channel_id=1, source_target_pairs={{0,1},{1,2},{2,3},{3,4},{4,5},{5,6},{6,7},{8,9},{9,10},{10,11},{11... | collective-permute-start | bytes 2949128 | tf_op jit(solution)/shard_map/ppermute | solution.py:16
  14.5 32.9 %collective-permute-done = f32[20,1,24,512]{3,2,1,0:T(8,128)} collective-permute-done((f32[20,1,24,512]{3,2,1,0:T(8,128)}, f32[20,1,24,512]{3,2,1,0:T(8,128)}, u32[]{:S(2)}, u32[]{:S(2)}) %collective-permute-start) | collective-permute-done | bytes 983072 | tf_op jit(solution)/shard_map/ppermute | solution.py:16
  48.3 2.4 multiply_add_fusion
  50.7 4.3 copy.87
  54.9 6.5 %reshape.1524 = f32[4,1,61440]{2,1,0:T(1,128)} reshape(f32[512,1,20,24]{3,2,1,0:T(8,128)} %bitcast.330) | data formatting | bytes 1966080
  61.5 4.1 all-to-all-start
  68.4 10.9 %all-to-all-done = f32[4,1,61440]{2,1,0:T(1,128)S(1)} async-done(((f32[4,1,61440]{2,1,0:T(1,128)}), f32[4,1,61440]{2,1,0:T(1,128)S(1)}, u32[]{:S(2)}, u32[]{:S(2)}) %all-to-all-start) | async-done | bytes 983072 | tf_op jit(solution)/shard_map/all_to_all | solution.py:134
  79.8 3.5 reduce.20
  83.3 6.0 %reshape.1525 = f32[512,1,20,24]{3,2,1,0:T(8,128)} reshape(f32[4,61440]{1,0:T(4,128)S(1)} %reduce.20) | data formatting | bytes 1966080
  89.4 5.6 %copy.88 = f32[20,1,24,512]{3,1,2,0:T(1,128)S(1)} copy(f32[20,1,24,512]{2,0,1,3:T(8,128)} %bitcast.331) | data formatting | bytes 1966080 | tf_op jit(solution)/shard_map/all_to_all | solution.py:134
  99.2 41.8 %psum.28 = f32[128,80]{0,1:T(8,128)S(1)} all-reduce(f32[128,80]{0,1:T(8,128)S(1)} %broadcast_select_fusion.3), channel_id=1, replica_groups=mesh['mem'=4,'sub'=8] {'mem','sub'}, use_global_device_ids=true, to_apply=%region_0.1 | all-reduce | flops 10240 | bytes 81920 | tf_op jit(solution)/shard_map/psum | solution.py:152
  143.0 11.7 %cholesky.74 = f32[128,128]{1,0:T(8,128)S(1)} custom-call(f32[128,128]{1,0:T(8,128)S(1)} %copy.93), custom_call_target="Cholesky" | custom-call | tf_op jit(solution)/shard_map/jit(cholesky)/cholesky | solution.py:69
  156.1 9.8 %custom-call.36 = f32[1,128,128]{1,2,0:T(8,128)S(1)} custom-call(f32[1,128,128]{2,1,0:T(8,128)S(1)} %get-tuple-element.21), custom_call_target="InvertDiagBlocksLowerTriangular" | custom-call | tf_op jit(solution)/shard_map/triangular_solve/custom-call.3 | solution.py:76
  166.1 9.8 %custom-call.35 = f32[1,128,128]{1,2,0:T(8,128)S(1)} custom-call(f32[1,128,128]{2,1,0:T(8,128)S(1)} %get-tuple-element.20), custom_call_target="InvertDiagBlocksLowerTriangular" | custom-call | tf_op jit(solution)/shard_map/triangular_solve/custom-call.2 | solution.py:72
  176.4 2.6 fusion.31
  179.3 2.8 fusion.186
  184.5 40.4 %psum.29 = f32[128,80]{0,1:T(8,128)S(1)} all-reduce(f32[128,80]{0,1:T(8,128)S(1)} %broadcast_select_fusion.2), channel_id=1, replica_groups=mesh['mem'=4,'sub'=8] {'mem','sub'}, use_global_device_ids=true, to_apply=%region_5.11 | all-reduce | flops 10240 | bytes 81920 | tf_op jit(solution)/shard_map/psum | solution.py:152
  225.5 11.7 %cholesky.85 = f32[128,128]{1,0:T(8,128)S(1)} custom-call(f32[128,128]{1,0:T(8,128)S(1)} %copy.98), custom_call_target="Cholesky" | custom-call | tf_op jit(solution)/shard_map/jit(cholesky)/cholesky | solution.py:69
  238.7 9.8 %custom-call.40 = f32[1,128,128]{1,2,0:T(8,128)S(1)} custom-call(f32[1,128,128]{2,1,0:T(8,128)S(1)} %get-tuple-element.19), custom_call_target="InvertDiagBlocksLowerTriangular" | custom-call | tf_op jit(solution)/shard_map/triangular_solve/custom-call.3 | solution.py:76
  248.7 9.8 %custom-call.39 = f32[1,128,128]{1,2,0:T(8,128)S(1)} custom-call(f32[1,128,128]{2,1,0:T(8,128)S(1)} %get-tuple-element.18), custom_call_target="InvertDiagBlocksLowerTriangular" | custom-call | tf_op jit(solution)/shard_map/triangular_solve/custom-call.2 | solution.py:72
  258.9 2.6 fusion.37
  266.2 40.3 %psum.30 = f32[128,80]{0,1:T(8,128)S(1)} all-reduce(f32[128,80]{0,1:T(8,128)S(1)} %broadcast_select_fusion.1), channel_id=1, replica_groups=mesh['mem'=4,'sub'=8] {'mem','sub'}, use_global_device_ids=true, to_apply=%region_8.14 | all-reduce | flops 10240 | bytes 81920 | tf_op jit(solution)/shard_map/psum | solution.py:152
  307.1 11.7 %cholesky.96 = f32[128,128]{1,0:T(8,128)S(1)} custom-call(f32[128,128]{1,0:T(8,128)S(1)} %copy.101), custom_call_target="Cholesky" | custom-call | tf_op jit(solution)/shard_map/jit(cholesky)/cholesky | solution.py:69
  320.2 9.8 %custom-call.44 = f32[1,128,128]{1,2,0:T(8,128)S(1)} custom-call(f32[1,128,128]{2,1,0:T(8,128)S(1)} %get-tuple-element.17), custom_call_target="InvertDiagBlocksLowerTriangular" | custom-call | tf_op jit(solution)/shard_map/triangular_solve/custom-call.3 | solution.py:76
  330.2 9.8 %custom-call.43 = f32[1,128,128]{1,2,0:T(8,128)S(1)} custom-call(f32[1,128,128]{2,1,0:T(8,128)S(1)} %get-tuple-element.16), custom_call_target="InvertDiagBlocksLowerTriangular" | custom-call | tf_op jit(solution)/shard_map/triangular_solve/custom-call.2 | solution.py:72
  340.4 2.6 fusion.35
  343.3 1.9 fusion.188
  347.7 40.6 %psum.31 = f32[128,80]{0,1:T(8,128)S(1)} all-reduce(f32[128,80]{0,1:T(8,128)S(1)} %broadcast_select_fusion), channel_id=1, replica_groups=mesh['mem'=4,'sub'=8] {'mem','sub'}, use_global_device_ids=true, to_apply=%region_11.17 | all-reduce | flops 10240 | bytes 81920 | tf_op jit(solution)/shard_map/psum | solution.py:152
  388.9 11.7 %cholesky.107 = f32[128,128]{1,0:T(8,128)S(1)} custom-call(f32[128,128]{1,0:T(8,128)S(1)} %copy.104), custom_call_target="Cholesky" | custom-call | tf_op jit(solution)/shard_map/jit(cholesky)/cholesky | solution.py:69
  402.2 9.8 %custom-call.48 = f32[1,128,128]{1,2,0:T(8,128)S(1)} custom-call(f32[1,128,128]{2,1,0:T(8,128)S(1)} %get-tuple-element.15), custom_call_target="InvertDiagBlocksLowerTriangular" | custom-call | tf_op jit(solution)/shard_map/triangular_solve/custom-call.3 | solution.py:76
  412.2 9.8 %custom-call.47 = f32[1,128,128]{1,2,0:T(8,128)S(1)} custom-call(f32[1,128,128]{2,1,0:T(8,128)S(1)} %get-tuple-element.14), custom_call_target="InvertDiagBlocksLowerTriangular" | custom-call | tf_op jit(solution)/shard_map/triangular_solve/custom-call.2 | solution.py:72
  422.4 2.6 fusion.33
  (161 shorter events, 41.5 us)
Async XLA Ops:
  0.0 14.1 %copy-start.8 = (f32[20,1,24,512]{3,2,1,0:T(8,128)S(1)}, f32[20,1,24,512]{3,2,1,0:T(8,128)}, u32[]{:S(2)}) copy-start(f32[20,1,24,512]{3,2,1,0:T(8,128)} %param.18) | copy-start | bytes 2949124
  0.0 47.4 %collective-permute-start = (f32[20,1,24,512]{3,2,1,0:T(8,128)}, f32[20,1,24,512]{3,2,1,0:T(8,128)}, u32[]{:S(2)}, u32[]{:S(2)}) collective-permute-start(f32[20,1,24,512]{3,2,1,0:T(8,128)} %param.18), channel_id=1, source_target_pairs={{0,1},{1,2},{2,3},{3,4},{4,5},{5,6},{6,7},{8,9},{9,10},{10,11},{11... | collective-permute-start | bytes 2949128 | tf_op jit(solution)/shard_map/ppermute | solution.py:16
  5.9 41.4 %collective-permute-start.1 = (f32[20,1,24,512]{3,2,1,0:T(8,128)}, f32[20,1,24,512]{3,2,1,0:T(8,128)S(1)}, u32[]{:S(2)}, u32[]{:S(2)}) collective-permute-start(f32[20,1,24,512]{3,2,1,0:T(8,128)} %param.18), channel_id=1, source_target_pairs={{1,0},{2,1},{3,2},{4,3},{5,4},{6,5},{7,6},{9,8},{10,9},{11,10},{12... | collective-permute-start | bytes 2949128 | tf_op jit(solution)/shard_map/ppermute | solution.py:17
  14.1 34.2 %copy-start.15 = (f32[1,512]{1,0:T(1,128)S(1)}, f32[1,512]{1,0:T(1,128)}, u32[]{:S(2)}) copy-start(f32[1,512]{1,0:T(1,128)} %param.21) | copy-start | bytes 6148
  47.4 0.9 copy-start.10
  61.5 6.4 %copy-start.28 = (f32[4,128]{1,0:T(4,128)S(1)}, f32[4,128]{1,0:T(4,128)}, u32[]{:S(2)}) copy-start(f32[4,128]{1,0:T(4,128)} %param.26) | copy-start | bytes 6148
  61.5 17.8 %all-to-all-start = ((f32[4,1,61440]{2,1,0:T(1,128)}), f32[4,1,61440]{2,1,0:T(1,128)S(1)}, u32[]{:S(2)}, u32[]{:S(2)}) async-start(f32[4,1,61440]{2,1,0:T(1,128)} %reshape.1524), calls=%async_computation | async-start | bytes 1966080 | tf_op jit(solution)/shard_map/all_to_all | solution.py:134
  94.9 0.9 copy-start.9
  95.9 1.0 copy-start.6
  97.7 1.5 copy-start.19
  97.7 44.8 %copy-start.27 = (f32[128]{0:T(128)S(1)}, f32[128]{0:T(128)}, u32[]{:S(2)}) copy-start(f32[128]{0:T(128)} %get-tuple-element.52) | copy-start | bytes 1540
  97.7 57.7 %copy-start.26 = (f32[128]{0:T(128)S(1)}, f32[128]{0:T(128)}, u32[]{:S(2)}) copy-start(f32[128]{0:T(128)} %get-tuple-element.49) | copy-start | bytes 1540
  99.1 76.8 %copy-start.13 = (f32[4,128]{1,0:T(4,128)S(1)}, f32[4,128]{1,0:T(4,128)}, u32[]{:S(2)}) copy-start(f32[4,128]{1,0:T(4,128)} %param.23) | copy-start | bytes 6148
  99.1 77.2 %copy-start.7 = (f32[4,20,1,24,128]{4,3,1,0,2:T(8,128)S(1)}, f32[4,20,1,24,128]{4,3,1,0,2:T(8,128)}, u32[]{:S(2)}) copy-start(f32[4,20,1,24,128]{4,3,1,0,2:T(8,128)} %copy-done.6) | copy-start | bytes 2949124
  182.1 0.9 copy-start.2
  183.0 0.8 copy-start.11
  183.9 0.7 copy-start.18
  183.9 41.1 %copy-start.25 = (f32[128]{0:T(128)S(1)}, f32[128]{0:T(128)}, u32[]{:S(2)}) copy-start(f32[128]{0:T(128)} %get-tuple-element.51) | copy-start | bytes 1540
  183.9 54.1 %copy-start.24 = (f32[128]{0:T(128)S(1)}, f32[128]{0:T(128)}, u32[]{:S(2)}) copy-start(f32[128]{0:T(128)} %get-tuple-element.48) | copy-start | bytes 1540
  183.9 75.0 %copy-start.12 = (f32[24,128]{1,0:T(8,128)S(1)}, f32[24,128]{1,0:T(8,128)}, u32[]{:S(2)}) copy-start(f32[24,128]{1,0:T(8,128)} %get-tuple-element.64) | copy-start | bytes 36868
  183.9 75.0 %copy-start.3 = (f32[80,24,128]{2,0,1:T(8,128)S(1)}, f32[80,24,128]{2,0,1:T(8,128)}, u32[]{:S(2)}) copy-start(f32[80,24,128]{2,0,1:T(8,128)} %copy-done.2) | copy-start | bytes 2949124
  263.7 0.9 copy-start.4
  265.5 0.7 copy-start.17
  265.5 41.0 %copy-start.23 = (f32[128]{0:T(128)S(1)}, f32[128]{0:T(128)}, u32[]{:S(2)}) copy-start(f32[128]{0:T(128)} %get-tuple-element.53) | copy-start | bytes 1540
  265.5 54.0 %copy-start.22 = (f32[128]{0:T(128)S(1)}, f32[128]{0:T(128)}, u32[]{:S(2)}) copy-start(f32[128]{0:T(128)} %get-tuple-element.47) | copy-start | bytes 1540
  265.5 74.9 %copy-start.5 = (f32[80,24,128]{2,0,1:T(8,128)S(1)}, f32[80,24,128]{2,0,1:T(8,128)}, u32[]{:S(2)}) copy-start(f32[80,24,128]{2,0,1:T(8,128)} %copy-done.4) | copy-start | bytes 2949124
  345.3 0.9 copy-start
  347.1 0.7 copy-start.16
  347.1 41.3 %copy-start.21 = (f32[128]{0:T(128)S(1)}, f32[128]{0:T(128)}, u32[]{:S(2)}) copy-start(f32[128]{0:T(128)} %get-tuple-element.50) | copy-start | bytes 1540
  347.1 54.3 %copy-start.20 = (f32[128]{0:T(128)S(1)}, f32[128]{0:T(128)}, u32[]{:S(2)}) copy-start(f32[128]{0:T(128)} %get-tuple-element.46) | copy-start | bytes 1540
  347.1 74.9 %copy-start.14 = (f32[4,128]{1,0:T(4,128)S(1)}, f32[4,128]{1,0:T(4,128)}, u32[]{:S(2)}) copy-start(f32[4,128]{1,0:T(4,128)} %param.23) | copy-start | bytes 6148
  347.1 75.3 %copy-start.1 = (f32[80,24,128]{2,0,1:T(8,128)S(1)}, f32[80,24,128]{2,0,1:T(8,128)}, u32[]{:S(2)}) copy-start(f32[80,24,128]{2,0,1:T(8,128)} %copy-done) | copy-start | bytes 2949124
where the time goes:
time: 432 us; the launch traced here: 428 us
  blocking collectives  163 us (38%)
  other arithmetic  145 us (34%)
  waiting for transfers between devices  43.8 us (10%)
  local copies, waits for them, and re-layouts  41.1 us (10%)
  matrix products  23.1 us (5%)
  starting transfers between devices  11.3 us (3%)
    psum x4, blocking collectives, shards(): lax.psum(local_prior(existing_grid_values, obs_rows[batch_index], obs_col...  163 us
    another operation x12, other arithmetic, obs_factors(): factor = jnp.linalg.cholesky(covariance)  49.7 us
    another operation x8, other arithmetic, obs_factors(): lax.linalg.triangular_solve(factor, midpoint_values, left_side=True, lowe...  42.2 us
    another operation x4, other arithmetic, obs_factors(): lax.linalg.triangular_solve(shifted, anomaly, left_side=True, lower=True)  39.2 us
    ppermute x1, waiting for transfers between devices, padded_2(): before = lax.ppermute(last, axis, up)  32.9 us
    unnamed x64, local copies, waits for them, and re-layouts  17.7 us
    all_to_all x1, waiting for transfers between devices, shards(): lax.all_to_all(propagated_grids, 'mem', split_axis=3, concat_axis=0, tile...  10.9 us
    dot_general x4, matrix products, apply_update(): jnp.einsum('mrcx,km->rcxk', anomaly, obs_anomaly, precision=highest)  10.5 us
  transfers between devices with their start and end apart: 3, of which 2 were waited for; matrix products, arithmetic and copies ran while one was open for 2% of the time, Pallas kernels for 0%

commit v1 on v0

--- a/solution.py
+++ b/solution.py
@@ -150,15 +150,18 @@
 
     for batch_index in range(batches):
         obs_prior = lax.psum(
-            local_prior(
-                existing_grid_values,
-                obs_rows[batch_index],
-                obs_cols[batch_index],
-                obs_weight[batch_index],
-                row_start,
-                col_start,
+            lax.psum(
+                local_prior(
+                    existing_grid_values,
+                    obs_rows[batch_index],
+                    obs_cols[batch_index],
+                    obs_weight[batch_index],
+                    row_start,
+                    col_start,
+                ),
+                "sub",
             ),
-            ("mem", "sub"),
+            "mem",
         )
         obs_anomaly, coeffs = obs_factors(obs_prior, obs_value[batch_index], obs_error[batch_index])
         existing_grid_values = apply_update(

time: 432 us -> 451 us (1.044)
  blocking collectives: 163 us -> 182 us
    psum x0 -> x4, blocking collectives: none -> 42.3 us  [shards(): lax.psum(lax.psum(local_prior(existing_grid_values, obs_rows[batch_index]...]
    psum x4, blocking collectives: 163 us -> 140 us  [shards(): lax.psum(local_prior(existing_grid_values, obs_rows[batch_index], obs_col...]
where the time goes in v1:
time: 451 us; the launch traced here: 447 us
  blocking collectives  182 us (40%)
  other arithmetic  145 us (32%)
  waiting for transfers between devices  43.8 us (10%)
  local copies, waits for them, and re-layouts  41.1 us (9%)
  matrix products  23.1 us (5%)
  starting transfers between devices  11.3 us (3%)
    psum x4, blocking collectives, shards(): lax.psum(local_prior(existing_grid_values, obs_rows[batch_index], obs_col...  140 us
    another operation x12, other arithmetic, obs_factors(): factor = jnp.linalg.cholesky(covariance)  49.7 us
    psum x4, blocking collectives, shards(): lax.psum(lax.psum(local_prior(existing_grid_values, obs_rows[batch_index]...  42.3 us
    another operation x8, other arithmetic, obs_factors(): lax.linalg.triangular_solve(factor, midpoint_values, left_side=True, lowe...  42.2 us
    another operation x4, other arithmetic, obs_factors(): lax.linalg.triangular_solve(shifted, anomaly, left_side=True, lower=True)  39.2 us
    ppermute x1, waiting for transfers between devices, padded_2(): before = lax.ppermute(last, axis, up)  32.9 us
    unnamed x64, local copies, waits for them, and re-layouts  17.7 us
    all_to_all x1, waiting for transfers between devices, shards(): lax.all_to_all(propagated_grids, 'mem', split_axis=3, concat_axis=0, tile...  10.9 us
  transfers between devices with their start and end apart: 3, of which 2 were waited for; matrix products, arithmetic and copies ran while one was open for 2% of the time, Pallas kernels for 0%

profile of v1, /device:TPU:0, one launch (start us, length us, event | category | flops | bytes accessed | tf_op | source)
XLA Modules:
  0.0 447.5 jit_solution(12589792750603687523)
XLA Ops:
  0.0 5.9 %collective-permute-start = (f32[20,1,24,512]{3,2,1,0:T(8,128)}, f32[20,1,24,512]{3,2,1,0:T(8,128)}, u32[]{:S(2)}, u32[]{:S(2)}) collective-permute-start(f32[20,1,24,512]{3,2,1,0:T(8,128)} %param.18), channel_id=1, source_target_pairs={{0,1},{1,2},{2,3},{3,4},{4,5},{5,6},{6,7},{8,9},{9,10},{10,11},{11... | collective-permute-start | bytes 2949128 | tf_op jit(solution)/shard_map/ppermute | solution.py:16
  14.5 32.9 %collective-permute-done = f32[20,1,24,512]{3,2,1,0:T(8,128)} collective-permute-done((f32[20,1,24,512]{3,2,1,0:T(8,128)}, f32[20,1,24,512]{3,2,1,0:T(8,128)}, u32[]{:S(2)}, u32[]{:S(2)}) %collective-permute-start) | collective-permute-done | bytes 983072 | tf_op jit(solution)/shard_map/ppermute | solution.py:16
  50.7 4.3 copy.87
  54.9 6.5 %reshape.1524 = f32[4,1,61440]{2,1,0:T(1,128)} reshape(f32[512,1,20,24]{3,2,1,0:T(8,128)} %bitcast.330) | data formatting | bytes 1966080
  61.5 4.1 all-to-all-start
  68.4 10.9 %all-to-all-done = f32[4,1,61440]{2,1,0:T(1,128)S(1)} async-done(((f32[4,1,61440]{2,1,0:T(1,128)}), f32[4,1,61440]{2,1,0:T(1,128)S(1)}, u32[]{:S(2)}, u32[]{:S(2)}) %all-to-all-start) | async-done | bytes 983072 | tf_op jit(solution)/shard_map/all_to_all | solution.py:134
  79.8 3.5 reduce.20
  83.3 6.0 %reshape.1525 = f32[512,1,20,24]{3,2,1,0:T(8,128)} reshape(f32[4,61440]{1,0:T(4,128)S(1)} %reduce.20) | data formatting | bytes 1966080
  89.4 5.6 %copy.88 = f32[20,1,24,512]{3,1,2,0:T(1,128)S(1)} copy(f32[20,1,24,512]{2,0,1,3:T(8,128)} %bitcast.331) | data formatting | bytes 1966080 | tf_op jit(solution)/shard_map/all_to_all | solution.py:134
  99.2 37.9 %psum.56 = f32[128,80]{0,1:T(8,128)S(1)} all-reduce(f32[128,80]{0,1:T(8,128)S(1)} %broadcast_select_fusion.3), channel_id=1, replica_groups=mesh['mem'=4,'sub'=8] {'sub'}, use_global_device_ids=true, to_apply=%region_0.1 | all-reduce | flops 10240 | bytes 81920 | tf_op jit(solution)/shard_map/psum | solution.py:153
  137.1 10.7 %psum.57 = f32[128,80]{0,1:T(8,128)S(1)} all-reduce(f32[128,80]{0,1:T(8,128)S(1)} %psum.56), channel_id=1, replica_groups=mesh['mem'=4,'sub'=8] {'mem'}, use_global_device_ids=true, to_apply=%region_1.2 | all-reduce | flops 10240 | bytes 81920 | tf_op jit(solution)/shard_map/psum | solution.py:152
  149.7 11.7 %cholesky.74 = f32[128,128]{1,0:T(8,128)S(1)} custom-call(f32[128,128]{1,0:T(8,128)S(1)} %copy.93), custom_call_target="Cholesky" | custom-call | tf_op jit(solution)/shard_map/jit(cholesky)/cholesky | solution.py:69
  162.8 9.8 %custom-call.36 = f32[1,128,128]{1,2,0:T(8,128)S(1)} custom-call(f32[1,128,128]{2,1,0:T(8,128)S(1)} %get-tuple-element.21), custom_call_target="InvertDiagBlocksLowerTriangular" | custom-call | tf_op jit(solution)/shard_map/triangular_solve/custom-call.3 | solution.py:76
  172.9 9.8 %custom-call.35 = f32[1,128,128]{1,2,0:T(8,128)S(1)} custom-call(f32[1,128,128]{2,1,0:T(8,128)S(1)} %get-tuple-element.20), custom_call_target="InvertDiagBlocksLowerTriangular" | custom-call | tf_op jit(solution)/shard_map/triangular_solve/custom-call.2 | solution.py:72
  186.0 2.8 fusion.186
  191.3 33.4 %psum.58 = f32[128,80]{0,1:T(8,128)S(1)} all-reduce(f32[128,80]{0,1:T(8,128)S(1)} %broadcast_select_fusion.2), channel_id=1, replica_groups=mesh['mem'=4,'sub'=8] {'sub'}, use_global_device_ids=true, to_apply=%region_6.12 | all-reduce | flops 10240 | bytes 81920 | tf_op jit(solution)/shard_map/psum | solution.py:153
  224.7 10.5 %psum.59 = f32[128,80]{0,1:T(8,128)S(1)} all-reduce(f32[128,80]{0,1:T(8,128)S(1)} %psum.58), channel_id=1, replica_groups=mesh['mem'=4,'sub'=8] {'mem'}, use_global_device_ids=true, to_apply=%region_7.13 | all-reduce | flops 10240 | bytes 81920 | tf_op jit(solution)/shard_map/psum | solution.py:152
  235.7 11.7 %cholesky.85 = f32[128,128]{1,0:T(8,128)S(1)} custom-call(f32[128,128]{1,0:T(8,128)S(1)} %copy.98), custom_call_target="Cholesky" | custom-call | tf_op jit(solution)/shard_map/jit(cholesky)/cholesky | solution.py:69
  248.9 9.8 %custom-call.40 = f32[1,128,128]{1,2,0:T(8,128)S(1)} custom-call(f32[1,128,128]{2,1,0:T(8,128)S(1)} %get-tuple-element.19), custom_call_target="InvertDiagBlocksLowerTriangular" | custom-call | tf_op jit(solution)/shard_map/triangular_solve/custom-call.3 | solution.py:76
  258.9 9.8 %custom-call.39 = f32[1,128,128]{1,2,0:T(8,128)S(1)} custom-call(f32[1,128,128]{2,1,0:T(8,128)S(1)} %get-tuple-element.18), custom_call_target="InvertDiagBlocksLowerTriangular" | custom-call | tf_op jit(solution)/shard_map/triangular_solve/custom-call.2 | solution.py:72
  276.4 35.3 %psum.60 = f32[128,80]{0,1:T(8,128)S(1)} all-reduce(f32[128,80]{0,1:T(8,128)S(1)} %broadcast_select_fusion.1), channel_id=1, replica_groups=mesh['mem'=4,'sub'=8] {'sub'}, use_global_device_ids=true, to_apply=%region_10.16 | all-reduce | flops 10240 | bytes 81920 | tf_op jit(solution)/shard_map/psum | solution.py:153
  311.7 10.5 %psum.61 = f32[128,80]{0,1:T(8,128)S(1)} all-reduce(f32[128,80]{0,1:T(8,128)S(1)} %psum.60), channel_id=1, replica_groups=mesh['mem'=4,'sub'=8] {'mem'}, use_global_device_ids=true, to_apply=%region_11.17 | all-reduce | flops 10240 | bytes 81920 | tf_op jit(solution)/shard_map/psum | solution.py:152
  322.8 11.7 %cholesky.96 = f32[128,128]{1,0:T(8,128)S(1)} custom-call(f32[128,128]{1,0:T(8,128)S(1)} %copy.101), custom_call_target="Cholesky" | custom-call | tf_op jit(solution)/shard_map/jit(cholesky)/cholesky | solution.py:69
  335.9 9.8 %custom-call.44 = f32[1,128,128]{1,2,0:T(8,128)S(1)} custom-call(f32[1,128,128]{2,1,0:T(8,128)S(1)} %get-tuple-element.17), custom_call_target="InvertDiagBlocksLowerTriangular" | custom-call | tf_op jit(solution)/shard_map/triangular_solve/custom-call.3 | solution.py:76
  346.0 9.8 %custom-call.43 = f32[1,128,128]{1,2,0:T(8,128)S(1)} custom-call(f32[1,128,128]{2,1,0:T(8,128)S(1)} %get-tuple-element.16), custom_call_target="InvertDiagBlocksLowerTriangular" | custom-call | tf_op jit(solution)/shard_map/triangular_solve/custom-call.2 | solution.py:72
  356.2 2.6 fusion.35
  363.5 33.4 %psum.62 = f32[128,80]{0,1:T(8,128)S(1)} all-reduce(f32[128,80]{0,1:T(8,128)S(1)} %broadcast_select_fusion), channel_id=1, replica_groups=mesh['mem'=4,'sub'=8] {'sub'}, use_global_device_ids=true, to_apply=%region_14.20 | all-reduce | flops 10240 | bytes 81920 | tf_op jit(solution)/shard_map/psum | solution.py:153
  396.8 10.5 %psum.63 = f32[128,80]{0,1:T(8,128)S(1)} all-reduce(f32[128,80]{0,1:T(8,128)S(1)} %psum.62), channel_id=1, replica_groups=mesh['mem'=4,'sub'=8] {'mem'}, use_global_device_ids=true, to_apply=%region_15.21 | all-reduce | flops 10240 | bytes 81920 | tf_op jit(solution)/shard_map/psum | solution.py:152
  407.9 11.7 %cholesky.107 = f32[128,128]{1,0:T(8,128)S(1)} custom-call(f32[128,128]{1,0:T(8,128)S(1)} %copy.104), custom_call_target="Cholesky" | custom-call | tf_op jit(solution)/shard_map/jit(cholesky)/cholesky | solution.py:69
  421.2 9.8 %custom-call.48 = f32[1,128,128]{1,2,0:T(8,128)S(1)} custom-call(f32[1,128,128]{2,1,0:T(8,128)S(1)} %get-tuple-element.15), custom_call_target="InvertDiagBlocksLowerTriangular" | custom-call | tf_op jit(solution)/shard_map/triangular_solve/custom-call.3 | solution.py:76
  431.2 9.8 %custom-call.47 = f32[1,128,128]{1,2,0:T(8,128)S(1)} custom-call(f32[1,128,128]{2,1,0:T(8,128)S(1)} %get-tuple-element.14), custom_call_target="InvertDiagBlocksLowerTriangular" | custom-call | tf_op jit(solution)/shard_map/triangular_solve/custom-call.2 | solution.py:72
  441.4 2.6 fusion.33
  (165 shorter events, 51.1 us)
Async XLA Ops:
  0.0 14.1 %copy-start.8 = (f32[20,1,24,512]{3,2,1,0:T(8,128)S(1)}, f32[20,1,24,512]{3,2,1,0:T(8,128)}, u32[]{:S(2)}) copy-start(f32[20,1,24,512]{3,2,1,0:T(8,128)} %param.18) | copy-start | bytes 2949124
  0.0 47.4 %collective-permute-start = (f32[20,1,24,512]{3,2,1,0:T(8,128)}, f32[20,1,24,512]{3,2,1,0:T(8,128)}, u32[]{:S(2)}, u32[]{:S(2)}) collective-permute-start(f32[20,1,24,512]{3,2,1,0:T(8,128)} %param.18), channel_id=1, source_target_pairs={{0,1},{1,2},{2,3},{3,4},{4,5},{5,6},{6,7},{8,9},{9,10},{10,11},{11... | collective-permute-start | bytes 2949128 | tf_op jit(solution)/shard_map/ppermute | solution.py:16
  5.9 41.4 %collective-permute-start.1 = (f32[20,1,24,512]{3,2,1,0:T(8,128)}, f32[20,1,24,512]{3,2,1,0:T(8,128)S(1)}, u32[]{:S(2)}, u32[]{:S(2)}) collective-permute-start(f32[20,1,24,512]{3,2,1,0:T(8,128)} %param.18), channel_id=1, source_target_pairs={{1,0},{2,1},{3,2},{4,3},{5,4},{6,5},{7,6},{9,8},{10,9},{11,10},{12... | collective-permute-start | bytes 2949128 | tf_op jit(solution)/shard_map/ppermute | solution.py:17
  14.1 34.2 %copy-start.15 = (f32[1,512]{1,0:T(1,128)S(1)}, f32[1,512]{1,0:T(1,128)}, u32[]{:S(2)}) copy-start(f32[1,512]{1,0:T(1,128)} %param.21) | copy-start | bytes 6148
  47.4 0.9 copy-start.10
  61.5 6.4 %copy-start.28 = (f32[4,128]{1,0:T(4,128)S(1)}, f32[4,128]{1,0:T(4,128)}, u32[]{:S(2)}) copy-start(f32[4,128]{1,0:T(4,128)} %param.26) | copy-start | bytes 6148
  61.5 17.8 %all-to-all-start = ((f32[4,1,61440]{2,1,0:T(1,128)}), f32[4,1,61440]{2,1,0:T(1,128)S(1)}, u32[]{:S(2)}, u32[]{:S(2)}) async-start(f32[4,1,61440]{2,1,0:T(1,128)} %reshape.1524), calls=%async_computation | async-start | bytes 1966080 | tf_op jit(solution)/shard_map/all_to_all | solution.py:134
  94.9 0.9 copy-start.9
  95.9 1.0 copy-start.6
  97.7 1.5 copy-start.19
  97.7 51.5 %copy-start.27 = (f32[128]{0:T(128)S(1)}, f32[128]{0:T(128)}, u32[]{:S(2)}) copy-start(f32[128]{0:T(128)} %get-tuple-element.52) | copy-start | bytes 1540
  97.7 64.4 %copy-start.26 = (f32[128]{0:T(128)S(1)}, f32[128]{0:T(128)}, u32[]{:S(2)}) copy-start(f32[128]{0:T(128)} %get-tuple-element.49) | copy-start | bytes 1540
  99.1 83.6 %copy-start.13 = (f32[4,128]{1,0:T(4,128)S(1)}, f32[4,128]{1,0:T(4,128)}, u32[]{:S(2)}) copy-start(f32[4,128]{1,0:T(4,128)} %param.23) | copy-start | bytes 6148
  99.1 84.0 %copy-start.7 = (f32[4,20,1,24,128]{4,3,1,0,2:T(8,128)S(1)}, f32[4,20,1,24,128]{4,3,1,0,2:T(8,128)}, u32[]{:S(2)}) copy-start(f32[4,20,1,24,128]{4,3,1,0,2:T(8,128)} %copy-done.6) | copy-start | bytes 2949124
  188.8 0.9 copy-start.2
  189.8 0.8 copy-start.11
  190.6 0.7 copy-start.18
  190.6 44.6 %copy-start.25 = (f32[128]{0:T(128)S(1)}, f32[128]{0:T(128)}, u32[]{:S(2)}) copy-start(f32[128]{0:T(128)} %get-tuple-element.51) | copy-start | bytes 1540
  190.6 57.6 %copy-start.24 = (f32[128]{0:T(128)S(1)}, f32[128]{0:T(128)}, u32[]{:S(2)}) copy-start(f32[128]{0:T(128)} %get-tuple-element.48) | copy-start | bytes 1540
  190.6 78.5 %copy-start.12 = (f32[24,128]{1,0:T(8,128)S(1)}, f32[24,128]{1,0:T(8,128)}, u32[]{:S(2)}) copy-start(f32[24,128]{1,0:T(8,128)} %get-tuple-element.64) | copy-start | bytes 36868
  190.7 78.5 %copy-start.3 = (f32[80,24,128]{2,0,1:T(8,128)S(1)}, f32[80,24,128]{2,0,1:T(8,128)}, u32[]{:S(2)}) copy-start(f32[80,24,128]{2,0,1:T(8,128)} %copy-done.2) | copy-start | bytes 2949124
  273.9 0.9 copy-start.4
  275.7 0.7 copy-start.17
  275.7 46.6 %copy-start.23 = (f32[128]{0:T(128)S(1)}, f32[128]{0:T(128)}, u32[]{:S(2)}) copy-start(f32[128]{0:T(128)} %get-tuple-element.53) | copy-start | bytes 1540
  275.7 59.5 %copy-start.22 = (f32[128]{0:T(128)S(1)}, f32[128]{0:T(128)}, u32[]{:S(2)}) copy-start(f32[128]{0:T(128)} %get-tuple-element.47) | copy-start | bytes 1540
  275.8 80.4 %copy-start.5 = (f32[80,24,128]{2,0,1:T(8,128)S(1)}, f32[80,24,128]{2,0,1:T(8,128)}, u32[]{:S(2)}) copy-start(f32[80,24,128]{2,0,1:T(8,128)} %copy-done.4) | copy-start | bytes 2949124
  361.0 0.9 copy-start
  362.8 0.7 copy-start.16
  362.8 44.6 %copy-start.21 = (f32[128]{0:T(128)S(1)}, f32[128]{0:T(128)}, u32[]{:S(2)}) copy-start(f32[128]{0:T(128)} %get-tuple-element.50) | copy-start | bytes 1540
  362.8 57.6 %copy-start.20 = (f32[128]{0:T(128)S(1)}, f32[128]{0:T(128)}, u32[]{:S(2)}) copy-start(f32[128]{0:T(128)} %get-tuple-element.46) | copy-start | bytes 1540
  362.8 78.2 %copy-start.14 = (f32[4,128]{1,0:T(4,128)S(1)}, f32[4,128]{1,0:T(4,128)}, u32[]{:S(2)}) copy-start(f32[4,128]{1,0:T(4,128)} %param.23) | copy-start | bytes 6148
  362.8 78.5 %copy-start.1 = (f32[80,24,128]{2,0,1:T(8,128)S(1)}, f32[80,24,128]{2,0,1:T(8,128)}, u32[]{:S(2)}) copy-start(f32[80,24,128]{2,0,1:T(8,128)} %copy-done) | copy-start | bytes 2949124
